TPU v7x, 32 devices: a whole 2x2x4 slice. The times are simulated.
32 devices in a mesh: gx: 2 (over y), gy: 4 (over x, core), gz: 4 (over z).
Axes of the slice: x: 2, y: 2, z: 4, core: 2. Of those that a mesh axis runs over, the one named last changes fastest.
Arguments:
- latent: float32 [32, 64, 2048], P('gx', 'gy', 'gz'), may hold values from -6 to 6
- conv_first: bfloat16 [3, 3, 192, 64], replicated, may hold values from -0.15625 to 0.15625
- conv_second: bfloat16 [3, 3, 192, 64], replicated, may hold values from -0.15625 to 0.15625
- time_weight: float32 [64, 64], replicated, may hold values from -0.75 to 0.75
- timesteps: int32 [4], replicated, may hold values from 1 to 999
- offsets: int32 [4, 3], replicated, may hold values from 0 to 1, as said below
Outputs:
- denoised: float32 [32, 64, 2048], P('gx', 'gy', 'gz')
Inputs may be any that keep to these rules, and one draw needn't show every extreme that they name: `offsets`: every entry is 0 or 1, and each of the three columns holds at least one 0 and at least one 1.
All inputs are finite; a program needn't handle non-finite values.
Results may differ from a plain program's by a relative error of at most 0.0055.
Values sent between devices are 32-bit elements; how exact they have to be, the bound alone decides.
No kernel may reach another device: no remote copies, remote signals or barrier semaphores. Data moves between devices by JAX's collectives and lax.ppermute only.
A program may use at most 64 MiB of HBM per device.

v0:
```python
import math

import jax
import jax.numpy as jnp
from jax import lax
from jax.experimental import pallas as pl
from jax.experimental.pallas import tpu as pltpu
from jax.sharding import PartitionSpec as P

SPAN = 4


def passed_along(value, axis, by):
    size = lax.axis_size(axis)
    return lax.ppermute(value, axis, [(i, (i + by) % size) for i in range(size)])


def time_biases(timesteps, time_weight):
    half_c = time_weight.shape[0] // 2
    freqs = jnp.exp(-math.log(10000.0) * jnp.arange(half_c, dtype=jnp.float32) / half_c)
    angles = timesteps.astype(jnp.float32)[:, None] * freqs[None, :]
    emb = jnp.concatenate([jnp.sin(angles), jnp.cos(angles)], axis=1)
    return jnp.dot(emb, time_weight, precision=lax.Precision.HIGHEST)


def banded(weight):
    taps_x, taps_y, depth, channels = weight.shape
    step = depth // 3
    columns = [
        jnp.pad(weight, ((0, 0), (0, 0), (j * step, (SPAN - 1 - j) * step), (0, 0))) for j in range(SPAN)
    ]
    return jnp.concatenate(columns, axis=3).reshape(taps_x * taps_y * (SPAN + 2) * step, SPAN * channels)


def step_kernel(cut_ref, delta_ref, block_ref, halo_ref, first_ref, second_ref, bias_ref, out_ref, in_ref, hid_ref):
    size_x, size_y, width = block_ref.shape
    band = first_ref.shape[1]
    channels = band // SPAN
    depth = band + 2 * channels
    groups = width // band
    half = size_x // 2
    cut = cut_ref[0]
    is_cut = cut == 1

    def spread(values):
        count = values.shape[0]
        edge = jnp.zeros((count, size_y, channels), jnp.float32)
        padded = jnp.concatenate([edge, values, edge], axis=2)
        row = lax.broadcasted_iota(jnp.int32, padded.shape, 1)
        before = jnp.where(row == 0, 0.0, pltpu.roll(padded, 1, 1))
        after = jnp.where(row == size_y - 1, 0.0, pltpu.roll(padded, size_y - 1, 1))
        return [v.astype(jnp.bfloat16) for v in (before, padded, after)]

    def put(ref, start, values):
        for tap, piece in enumerate(spread(values)):
            ref[tap, pl.ds(start, values.shape[0])] = piece

    def convolve(ref, start, count, weight_ref, group):
        total = None
        lanes = pl.ds(group * band, depth)
        for tap_x in range(3):
            for tap_y in range(3):
                rows = ref[tap_y, pl.ds(start + tap_x, count), :, lanes].reshape(count * size_y, depth)
                tap = tap_x * 3 + tap_y
                part = jnp.dot(rows, weight_ref[pl.ds(tap * depth, depth), :], preferred_element_type=jnp.float32)
                total = part if total is None else total + part
        return total

    blank = jnp.zeros((3, 1, size_y, width + 2 * channels), jnp.bfloat16)
    in_ref[:, pl.ds(half + 2, 1)] = blank
    put(in_ref, 0, jnp.where(is_cut, halo_ref[pl.ds(0, 2)], 0.0))
    put(in_ref, 2, block_ref[pl.ds(0, half)])
    put(in_ref, half + 2 + cut, block_ref[pl.ds(half, half)])
    put(in_ref, size_x + 2 + cut, jnp.where(is_cut, halo_ref[pl.ds(2, 2)], 0.0))

    hid_ref[:, pl.ds(half + 1, 1)] = blank
    for side in range(2):
        start = 0 if side == 0 else half + 1 + cut
        pieces = []
        for group in range(groups):
            value = convolve(in_ref, start, half + 1, first_ref, group) + bias_ref[...]
            pieces.append(value / (1.0 + jnp.exp(-value)))
        hidden = jnp.concatenate(pieces, axis=1).reshape(half + 1, size_y, width)
        plane = lax.broadcasted_iota(jnp.int32, hidden.shape, 0)
        hidden = jnp.where((plane != (0 if side == 0 else half)) | is_cut, hidden, 0.0)
        put(hid_ref, start, hidden)

    for side in range(2):
        start = 0 if side == 0 else half + cut
        for group in range(groups):
            noise = convolve(hid_ref, start, half, second_ref, group).reshape(half, size_y, band)
            where = (pl.ds(side * half, half), slice(None), pl.ds(group * band, band))
            out_ref[where] = block_ref[where] + delta_ref[0] * noise


def denoise(block, halo, cut, delta, first, second, bias):
    size_x, size_y, width = block.shape
    channels = bias.shape[1] // SPAN
    smem = pl.BlockSpec(memory_space=pltpu.SMEM)
    vmem = pl.BlockSpec(memory_space=pltpu.VMEM)
    return pl.pallas_call(
        step_kernel,
        out_shape=jax.ShapeDtypeStruct(block.shape, jnp.float32),
        in_specs=[smem, smem, vmem, vmem, vmem, vmem, vmem],
        out_specs=vmem,
        scratch_shapes=[
            pltpu.VMEM((3, size_x + 5, size_y, width + 2 * channels), jnp.bfloat16),
            pltpu.VMEM((3, size_x + 3, size_y, width + 2 * channels), jnp.bfloat16),
        ],
        compiler_params=pltpu.CompilerParams(vmem_limit_bytes=32 << 20),
        name="denoise",
    )(cut, delta, block, halo, first, second, bias)


def slide(block, move, axis_name, axis):
    half = block.shape[axis] // 2
    lower = lax.slice_in_dim(block, 0, half, axis=axis)
    upper = lax.slice_in_dim(block, half, 2 * half, axis=axis)
    if move < 0:
        return jnp.concatenate([passed_along(upper, axis_name, 1), lower], axis)
    return jnp.concatenate([upper, passed_along(lower, axis_name, -1)], axis)


def fetch_halo(block):
    length = block.shape[0]
    size = lax.axis_size("gx")
    if size == 2:
        ends = jnp.concatenate([block[length - 2 :], block[:2]], 0)
        return passed_along(ends, "gx", 1)
    return jnp.concatenate([passed_along(block[length - 2 :], "gx", 1), passed_along(block[:2], "gx", -1)], 0)


def exchange(block, move_y, move_z, cut):
    def branch(y, z, x):
        def run(values):
            if z:
                values = slide(values, z, "gz", 2)
            if y:
                values = slide(values, y, "gy", 1)
            if x is None:
                return values
            halo = fetch_halo(values) if x else jnp.zeros((4,) + values.shape[1:], jnp.float32)
            return values, halo

        return run

    moves = (-1, 0, 1)
    if cut is None:
        branches = [branch(y, z, None) for y in moves for z in moves]
        return lax.switch((move_y + 1) * 3 + move_z + 1, branches, block)
    branches = [branch(y, z, x) for y in moves for z in moves for x in (0, 1)]
    return lax.switch(((move_y + 1) * 3 + move_z + 1) * 2 + cut, branches, block)


def shards(latent, conv_first, conv_second, time_weight, timesteps, offsets):
    count = timesteps.shape[0]
    first, second = banded(conv_first), banded(conv_second)
    bias = jnp.tile(time_biases(timesteps, time_weight), (1, SPAN))
    later = jnp.concatenate([timesteps[1:], jnp.zeros((1,), jnp.int32)])
    deltas = (later - timesteps).astype(jnp.float32) / 1000.0
    edge = jnp.zeros((1, 3), jnp.int32)
    moves = jnp.concatenate([offsets, edge]) - jnp.concatenate([edge, offsets])
    block = latent
    for step in range(count):
        cut = offsets[step, 0]
        block, halo = exchange(block, moves[step, 1], moves[step, 2], cut)
        block = denoise(
            block, halo, cut[None], deltas[step : step + 1], first, second, bias[step : step + 1]
        )
    return exchange(block, moves[count, 1], moves[count, 2], None)


def solution(mesh):
    return jax.shard_map(
        shards,
        mesh=mesh,
        in_specs=(P("gx", "gy", "gz"), P(), P(), P(), P(), P()),
        out_specs=P("gx", "gy", "gz"),
        check_vma=False,
    )
```

profile of v0, /device:TPU:0, one launch (start us, length us, event | category | flops | bytes accessed | tf_op | source)
XLA Modules:
  0.0 108.8 jit_solution(1042839141209602997)
XLA Ops:
  0.0 0.0 copy-start
  0.0 0.8 pad_subtract_fusion
  0.8 0.7 fusion.209
  2.7 1.4 %fusion.210 = (s32[1,1]{1,0:T(1,128)}, s32[1,1]{1,0:T(1,128)}, s32[1,1]{1,0:T(1,128)}, s32[1,1]{1,0:T(1,128)}) fusion(s32[4,3]{1,0:T(4,128)} %param.92), kind=kLoop, calls=%fused_computation.519 | loop fusion | bytes 32 | tf_op jit(solution)/shard_map/slice | solution.py:165
  4.1 0.7 slice.952
  4.8 0.7 fusion.123
  5.6 0.7 fusion.211
  13.8 0.0 copy-start.7
  13.8 9.2 %conditional.5 = (f32[16,16,512]{2,1,0:T(8,128)}, f32[4,16,512]{2,1,0:T(8,128)}) conditional(s32[]{:T(128)} %bitcast.8, f32[16,16,512]{2,1,0:T(8,128)} %param.87, f32[16,16,512]{2,1,0:T(8,128)} %param.87, f32[16,16,512]{2,1,0:T(8,128)} %param.87, f32[16,16,512]{2,1,0:T(8,128)} %param.87, ...), branch_computations={%region_0.1_spmd, %region_1.2_spmd, %region_2.3_spmd, %region_3.4_... | conditional | flops 360448 | bytes 6684808 | solution.py:152
  13.9 1.1 %fusion.140 = (f32[16,8,512]{2,1,0:T(8,128)S(1)}, f32[16,8,512]{2,1,0:T(8,128)S(1)}) fusion(f32[16,16,512]{2,1,0:T(8,128)} %param.14), kind=kLoop, calls=%fused_computation.449 | loop fusion | bytes 1048576 | tf_op jit(solution)/shard_map/cond/branch_14_fun/slice | solution.py:118
  15.0 2.5 %collective-permute-start.25 = (f32[16,8,512]{2,1,0:T(8,128)S(1)}, f32[16,8,512]{2,1,0:T(8,128)S(1)}, u32[]{:S(2)}, u32[]{:S(2)}) collective-permute-start(f32[16,8,512]{2,1,0:T(8,128)S(1)} %get-tuple-element.156), channel_id=1, source_target_pairs={{0,12},{4,0},{8,4},{12,8},{1,13},{5,1},{9,5},{13,9},{2,14},{6,2},{... | collective-permute-start | bytes 786440 | tf_op jit(solution)/shard_map/cond/branch_14_fun/ppermute | solution.py:15
  17.4 3.9 %collective-permute-done.25 = f32[16,8,512]{2,1,0:T(8,128)S(1)} collective-permute-done((f32[16,8,512]{2,1,0:T(8,128)S(1)}, f32[16,8,512]{2,1,0:T(8,128)S(1)}, u32[]{:S(2)}, u32[]{:S(2)}) %collective-permute-start.25) | collective-permute-done | bytes 262176 | tf_op jit(solution)/shard_map/cond/branch_14_fun/ppermute | solution.py:15
  21.3 0.8 pad_maximum_fusion.21
  22.1 0.7 broadcast.109
  23.0 0.0 copy-done.7
  23.0 3.5 %fusion.114 = bf16[3,3,384,256]{2,3,1,0:T(8,128)(2,1)} fusion(bf16[3,3,192,64]{2,3,1,0:T(8,128)(2,1)S(1)} %copy-done.7), kind=kLoop, calls=%fused_computation.414 | loop fusion | flops 17694720 | bytes 1990656 | tf_op jit(solution)/shard_map/concatenate | solution.py:32
  26.5 0.0 copy-start.8
  26.5 2.7 %copy.16 = bf16[3,3,384,256]{3,2,1,0:T(8,128)(2,1)S(1)} copy(bf16[3,3,384,256]{2,3,1,0:T(8,128)(2,1)} %fusion.114) | data formatting | bytes 3538944 | tf_op jit(solution)/shard_map/concatenate | solution.py:32
  29.2 0.0 copy-done.8
  29.2 3.5 %fusion.117 = bf16[3,3,384,256]{2,3,1,0:T(8,128)(2,1)} fusion(bf16[3,3,192,64]{2,3,1,0:T(8,128)(2,1)S(1)} %copy-done.8), kind=kLoop, calls=%fused_computation.417 | loop fusion | flops 17694720 | bytes 1990656 | tf_op jit(solution)/shard_map/concatenate | solution.py:32
  32.7 0.0 copy-start.9
  32.7 3.8 %copy.17 = bf16[3,3,384,256]{3,2,1,0:T(8,128)(2,1)} copy(bf16[3,3,384,256]{2,3,1,0:T(8,128)(2,1)} %fusion.117) | data formatting | bytes 3538944 | tf_op jit(solution)/shard_map/concatenate | solution.py:32
  36.6 0.0 copy-done.9
  36.6 0.1 multiply_sine_fusion
  36.7 0.0 copy-done
  36.7 0.2 fusion.118
  37.0 0.1 tile.22.bias_ref
  37.0 0.0 copy-start.2
  37.0 1.5 %copy-done.2 = bf16[3,3,384,256]{3,2,1,0:T(8,128)(2,1)S(1)} copy-done((bf16[3,3,384,256]{3,2,1,0:T(8,128)(2,1)S(1)}, bf16[3,3,384,256]{3,2,1,0:T(8,128)(2,1)}, u32[]{:S(2)}) %copy-start.2) | copy-done | bytes 1769496
  38.5 5.7 %denoise.4 = f32[16,16,512]{2,1,0:T(8,128)S(1)} custom-call(s32[1]{0:T(128)} %bitcast.7.cut_ref, f32[1]{0:T(128)} %get-tuple-element.385.delta_ref, f32[16,16,512]{2,1,0:T(8,128)} %get-tuple-element.104.block_ref, f32[4,16,512]{2,1,0:T(8,128)} %get-tuple-element.105.halo_ref, bf16[3456,256]{1,0:T(8,128)(2,1)S(1)} %bitcast.20, ...), custom_call_target="tpu_custom_call" | custom-call | tf_op jit(solution)/shard_map/denoise/pallas_call | solution.py:101
  44.2 16.1 %conditional.6 = (f32[16,16,512]{2,1,0:T(8,128)}, f32[4,16,512]{2,1,0:T(8,128)}) conditional(s32[]{:T(128)} %bitcast.6, f32[16,16,512]{2,1,0:T(8,128)S(1)} %denoise.4, f32[16,16,512]{2,1,0:T(8,128)S(1)} %denoise.4, f32[16,16,512]{2,1,0:T(8,128)S(1)} %denoise.4, f32[16,16,512]{2,1,0:T(8,128)S(1)} %denoise.4, ...), branch_computations={%region_18.19_spmd, %region_19.20_spmd, %region_20.21_spmd, %regio... | conditional | flops 360448 | bytes 6684808 | solution.py:152
  44.3 0.1 fusion.156
  44.3 3.7 %collective-permute-start.51 = (f32[16,16,256]{2,1,0:T(8,128)S(1)}, f32[16,16,256]{2,1,0:T(8,128)S(1)}, u32[]{:S(2)}, u32[]{:S(2)}) collective-permute-start(f32[16,16,256]{2,1,0:T(8,128)S(1)} %get-tuple-element.202), channel_id=1, source_target_pairs={{0,3},{1,0},{2,1},{3,2},{4,7},{5,4},{6,5},{7,6},{8,11},{9,8},{10,9... | collective-permute-start | bytes 786440 | tf_op jit(solution)/shard_map/cond/branch_11_fun/ppermute | solution.py:15
  48.0 6.6 %collective-permute-done.51 = f32[16,16,256]{2,1,0:T(8,128)S(1)} collective-permute-done((f32[16,16,256]{2,1,0:T(8,128)S(1)}, f32[16,16,256]{2,1,0:T(8,128)S(1)}, u32[]{:S(2)}, u32[]{:S(2)}) %collective-permute-start.51) | collective-permute-done | bytes 262176 | tf_op jit(solution)/shard_map/cond/branch_11_fun/ppermute | solution.py:15
  54.6 1.6 %collective-permute-start.52 = (f32[4,16,512]{2,1,0:T(8,128)S(1)}, f32[4,16,512]{2,1,0:T(8,128)}, u32[]{:S(2)}, u32[]{:S(2)}) collective-permute-start(f32[4,16,512]{2,1,0:T(8,128)S(1)} %pad_maximum_fusion.44), channel_id=1, source_target_pairs={{0,16},{16,0},{1,17},{17,1},{2,18},{18,2},{3,19},{19,3},{4,20},{20... | collective-permute-start | bytes 393224 | tf_op jit(solution)/shard_map/cond/branch_11_fun/ppermute | solution.py:15
  56.2 0.9 pad_maximum_fusion.43
  57.0 3.1 %collective-permute-done.52 = f32[4,16,512]{2,1,0:T(8,128)} collective-permute-done((f32[4,16,512]{2,1,0:T(8,128)S(1)}, f32[4,16,512]{2,1,0:T(8,128)}, u32[]{:S(2)}, u32[]{:S(2)}) %collective-permute-start.52) | collective-permute-done | bytes 131104 | tf_op jit(solution)/shard_map/cond/branch_11_fun/ppermute | solution.py:15
  60.4 0.1 tile.24.bias_ref
  60.4 0.0 copy-start.3
  60.5 1.5 %copy-done.3 = bf16[3,3,384,256]{3,2,1,0:T(8,128)(2,1)S(1)} copy-done((bf16[3,3,384,256]{3,2,1,0:T(8,128)(2,1)S(1)}, bf16[3,3,384,256]{3,2,1,0:T(8,128)(2,1)}, u32[]{:S(2)}) %copy-start.3) | copy-done | bytes 1769496
  61.9 5.8 %denoise.5 = f32[16,16,512]{2,1,0:T(8,128)S(1)} custom-call(s32[1]{0:T(128)} %bitcast.5.cut_ref, f32[1]{0:T(128)} %get-tuple-element.386.delta_ref, f32[16,16,512]{2,1,0:T(8,128)} %get-tuple-element.106.block_ref, f32[4,16,512]{2,1,0:T(8,128)} %get-tuple-element.107.halo_ref, bf16[3456,256]{1,0:T(8,128)(2,1)S(1)} %bitcast.21, ...), custom_call_target="tpu_custom_call" | custom-call | tf_op jit(solution)/shard_map/denoise/pallas_call | solution.py:101
  67.7 22.8 %conditional.7 = (f32[16,16,512]{2,1,0:T(8,128)}, f32[4,16,512]{2,1,0:T(8,128)}) conditional(s32[]{:T(128)} %bitcast.4, f32[16,16,512]{2,1,0:T(8,128)S(1)} %denoise.5, f32[16,16,512]{2,1,0:T(8,128)S(1)} %denoise.5, f32[16,16,512]{2,1,0:T(8,128)S(1)} %denoise.5, f32[16,16,512]{2,1,0:T(8,128)S(1)} %denoise.5, ...), branch_computations={%region_36.37_spmd, %region_37.38_spmd, %region_38.39_spmd, %regio... | conditional | flops 360448 | bytes 6684808 | solution.py:152
  67.7 0.1 fusion.165
  67.8 0.5 collective-permute-start.68
  68.3 9.4 %collective-permute-done.68 = f32[16,16,256]{2,1,0:T(8,128)S(1)} collective-permute-done((f32[16,16,256]{2,1,0:T(8,128)S(1)}, f32[16,16,256]{2,1,0:T(8,128)S(1)}, u32[]{:S(2)}, u32[]{:S(2)}) %collective-permute-start.68) | collective-permute-done | bytes 262176 | tf_op jit(solution)/shard_map/cond/branch_1_fun/ppermute | solution.py:15
  77.8 0.1 collective-permute-start.69
  77.8 5.8 %collective-permute-done.69 = f32[16,8,512]{2,1,0:T(8,128)S(1)} collective-permute-done((f32[16,8,512]{2,1,0:T(8,128)S(1)}, f32[16,8,512]{2,1,0:T(8,128)S(1)}, u32[]{:S(2)}, u32[]{:S(2)}) %collective-permute-start.69) | collective-permute-done | bytes 262176 | tf_op jit(solution)/shard_map/cond/branch_1_fun/ppermute | solution.py:15
  83.6 0.8 fusion.50
  84.4 0.9 fusion.164
  85.4 1.6 %collective-permute-start.70 = (f32[4,16,512]{2,1,0:T(8,128)S(1)}, f32[4,16,512]{2,1,0:T(8,128)}, u32[]{:S(2)}, u32[]{:S(2)}) collective-permute-start(f32[4,16,512]{2,1,0:T(8,128)S(1)} %pad_maximum_fusion.60), channel_id=1, source_target_pairs={{0,16},{16,0},{1,17},{17,1},{2,18},{18,2},{3,19},{19,3},{4,20},{20... | collective-permute-start | bytes 393224 | tf_op jit(solution)/shard_map/cond/branch_1_fun/ppermute | solution.py:15
  86.9 3.6 %collective-permute-done.70 = f32[4,16,512]{2,1,0:T(8,128)} collective-permute-done((f32[4,16,512]{2,1,0:T(8,128)S(1)}, f32[4,16,512]{2,1,0:T(8,128)}, u32[]{:S(2)}, u32[]{:S(2)}) %collective-permute-start.70) | collective-permute-done | bytes 131104 | tf_op jit(solution)/shard_map/cond/branch_1_fun/ppermute | solution.py:15
  90.5 0.1 tile.26.bias_ref
  90.6 0.0 copy-start.4
  90.6 1.5 %copy-done.4 = bf16[3,3,384,256]{3,2,1,0:T(8,128)(2,1)S(1)} copy-done((bf16[3,3,384,256]{3,2,1,0:T(8,128)(2,1)S(1)}, bf16[3,3,384,256]{3,2,1,0:T(8,128)(2,1)}, u32[]{:S(2)}) %copy-start.4) | copy-done | bytes 1769496
  92.1 5.7 %denoise.6 = f32[16,16,512]{2,1,0:T(8,128)S(1)} custom-call(s32[1]{0:T(128)} %bitcast.3.cut_ref, f32[1]{0:T(128)} %get-tuple-element.387.delta_ref, f32[16,16,512]{2,1,0:T(8,128)} %get-tuple-element.108.block_ref, f32[4,16,512]{2,1,0:T(8,128)} %get-tuple-element.109.halo_ref, bf16[3456,256]{1,0:T(8,128)(2,1)S(1)} %bitcast.22, ...), custom_call_target="tpu_custom_call" | custom-call | tf_op jit(solution)/shard_map/denoise/pallas_call | solution.py:101
  97.8 1.7 %conditional.8 = (f32[16,16,512]{2,1,0:T(8,128)}, f32[4,16,512]{2,1,0:T(8,128)}) conditional(s32[]{:T(128)} %bitcast.2, f32[16,16,512]{2,1,0:T(8,128)S(1)} %denoise.6, f32[16,16,512]{2,1,0:T(8,128)S(1)} %denoise.6, f32[16,16,512]{2,1,0:T(8,128)S(1)} %denoise.6, f32[16,16,512]{2,1,0:T(8,128)S(1)} %denoise.6, ...), branch_computations={%region_54.55_spmd, %region_55.56_spmd, %region_56.57_spmd, %regio... | conditional | flops 360448 | bytes 6684808 | solution.py:152
  97.8 0.8 copy.142
  98.6 0.7 broadcast.133
  99.5 0.1 tile.28.bias_ref
  99.6 1.5 %copy-done.5 = bf16[3,3,384,256]{3,2,1,0:T(8,128)(2,1)S(1)} copy-done((bf16[3,3,384,256]{3,2,1,0:T(8,128)(2,1)S(1)}, bf16[3,3,384,256]{3,2,1,0:T(8,128)(2,1)}, u32[]{:S(2)}) %copy-start.5) | copy-done | bytes 1769496
  101.1 5.6 %denoise.7 = f32[16,16,512]{2,1,0:T(8,128)S(1)} custom-call(s32[1]{0:T(128)} %bitcast.1.cut_ref, f32[1]{0:T(128)} %get-tuple-element.388.delta_ref, f32[16,16,512]{2,1,0:T(8,128)} %get-tuple-element.110.block_ref, f32[4,16,512]{2,1,0:T(8,128)} %get-tuple-element.111.halo_ref, bf16[3456,256]{1,0:T(8,128)(2,1)S(1)} %bitcast.23, ...), custom_call_target="tpu_custom_call" | custom-call | tf_op jit(solution)/shard_map/denoise/pallas_call | solution.py:101
  106.8 0.0 copy-start.6
  106.8 0.8 copy-done.6
  107.6 0.8 copy-done.1
  (14 shorter events, 0.1 us)
Async XLA Ops:
  0.0 36.7 %copy-start = (f32[64,64]{1,0:T(8,128)S(1)}, f32[64,64]{1,0:T(8,128)}, u32[]{:S(2)}) copy-start(f32[64,64]{1,0:T(8,128)} %param.90) | copy-start | bytes 49156
  13.8 9.2 %copy-start.7 = (bf16[3,3,192,64]{2,3,1,0:T(8,128)(2,1)S(1)}, bf16[3,3,192,64]{2,3,1,0:T(8,128)(2,1)}, u32[]{:S(2)}) copy-start(bf16[3,3,192,64]{2,3,1,0:T(8,128)(2,1)} %param.88) | copy-start | bytes 663556
  15.0 6.3 %collective-permute-start.25 = (f32[16,8,512]{2,1,0:T(8,128)S(1)}, f32[16,8,512]{2,1,0:T(8,128)S(1)}, u32[]{:S(2)}, u32[]{:S(2)}) collective-permute-start(f32[16,8,512]{2,1,0:T(8,128)S(1)} %get-tuple-element.156), channel_id=1, source_target_pairs={{0,12},{4,0},{8,4},{12,8},{1,13},{5,1},{9,5},{13,9},{2,14},{6,2},{... | collective-permute-start | bytes 786440 | tf_op jit(solution)/shard_map/cond/branch_14_fun/ppermute | solution.py:15
  26.5 2.7 %copy-start.8 = (bf16[3,3,192,64]{2,3,1,0:T(8,128)(2,1)S(1)}, bf16[3,3,192,64]{2,3,1,0:T(8,128)(2,1)}, u32[]{:S(2)}) copy-start(bf16[3,3,192,64]{2,3,1,0:T(8,128)(2,1)} %param.89) | copy-start | bytes 663556
  32.7 3.9 %copy-start.9 = (s32[4]{0:T(128)S(1)}, s32[4]{0:T(128)}, u32[]{:S(2)}) copy-start(s32[4]{0:T(128)} %param.91) | copy-start | bytes 52
  37.0 1.5 %copy-start.2 = (bf16[3,3,384,256]{3,2,1,0:T(8,128)(2,1)S(1)}, bf16[3,3,384,256]{3,2,1,0:T(8,128)(2,1)}, u32[]{:S(2)}) copy-start(bf16[3,3,384,256]{3,2,1,0:T(8,128)(2,1)} %copy.17) | copy-start | bytes 5308420
  44.3 10.2 %collective-permute-start.51 = (f32[16,16,256]{2,1,0:T(8,128)S(1)}, f32[16,16,256]{2,1,0:T(8,128)S(1)}, u32[]{:S(2)}, u32[]{:S(2)}) collective-permute-start(f32[16,16,256]{2,1,0:T(8,128)S(1)} %get-tuple-element.202), channel_id=1, source_target_pairs={{0,3},{1,0},{2,1},{3,2},{4,7},{5,4},{6,5},{7,6},{8,11},{9,8},{10,9... | collective-permute-start | bytes 786440 | tf_op jit(solution)/shard_map/cond/branch_11_fun/ppermute | solution.py:15
  54.6 5.6 %collective-permute-start.52 = (f32[4,16,512]{2,1,0:T(8,128)S(1)}, f32[4,16,512]{2,1,0:T(8,128)}, u32[]{:S(2)}, u32[]{:S(2)}) collective-permute-start(f32[4,16,512]{2,1,0:T(8,128)S(1)} %pad_maximum_fusion.44), channel_id=1, source_target_pairs={{0,16},{16,0},{1,17},{17,1},{2,18},{18,2},{3,19},{19,3},{4,20},{20... | collective-permute-start | bytes 393224 | tf_op jit(solution)/shard_map/cond/branch_11_fun/ppermute | solution.py:15
  60.4 1.5 %copy-start.3 = (bf16[3,3,384,256]{3,2,1,0:T(8,128)(2,1)S(1)}, bf16[3,3,384,256]{3,2,1,0:T(8,128)(2,1)}, u32[]{:S(2)}) copy-start(bf16[3,3,384,256]{3,2,1,0:T(8,128)(2,1)} %copy.17) | copy-start | bytes 5308420
  67.8 9.9 %collective-permute-start.68 = (f32[16,16,256]{2,1,0:T(8,128)S(1)}, f32[16,16,256]{2,1,0:T(8,128)S(1)}, u32[]{:S(2)}, u32[]{:S(2)}) collective-permute-start(f32[16,16,256]{2,1,0:T(8,128)S(1)} %get-tuple-element.233), channel_id=1, source_target_pairs={{0,1},{1,2},{2,3},{3,0},{4,5},{5,6},{6,7},{7,4},{8,9},{9,10},{10,1... | collective-permute-start | bytes 786440 | tf_op jit(solution)/shard_map/cond/branch_1_fun/ppermute | solution.py:15
  77.8 5.8 %collective-permute-start.69 = (f32[16,8,512]{2,1,0:T(8,128)S(1)}, f32[16,8,512]{2,1,0:T(8,128)S(1)}, u32[]{:S(2)}, u32[]{:S(2)}) collective-permute-start(f32[16,8,512]{2,1,0:T(8,128)S(1)} %fusion.51), channel_id=1, source_target_pairs={{0,4},{4,8},{8,12},{12,0},{1,5},{5,9},{9,13},{13,1},{2,6},{6,10},{... | collective-permute-start | bytes 786440 | tf_op jit(solution)/shard_map/cond/branch_1_fun/ppermute | solution.py:15
  85.4 5.1 %collective-permute-start.70 = (f32[4,16,512]{2,1,0:T(8,128)S(1)}, f32[4,16,512]{2,1,0:T(8,128)}, u32[]{:S(2)}, u32[]{:S(2)}) collective-permute-start(f32[4,16,512]{2,1,0:T(8,128)S(1)} %pad_maximum_fusion.60), channel_id=1, source_target_pairs={{0,16},{16,0},{1,17},{17,1},{2,18},{18,2},{3,19},{19,3},{4,20},{20... | collective-permute-start | bytes 393224 | tf_op jit(solution)/shard_map/cond/branch_1_fun/ppermute | solution.py:15
  90.6 1.5 %copy-start.4 = (bf16[3,3,384,256]{3,2,1,0:T(8,128)(2,1)S(1)}, bf16[3,3,384,256]{3,2,1,0:T(8,128)(2,1)}, u32[]{:S(2)}) copy-start(bf16[3,3,384,256]{3,2,1,0:T(8,128)(2,1)} %copy.17) | copy-start | bytes 5308420
  99.6 1.5 %copy-start.5 = (bf16[3,3,384,256]{3,2,1,0:T(8,128)(2,1)S(1)}, bf16[3,3,384,256]{3,2,1,0:T(8,128)(2,1)}, u32[]{:S(2)}) copy-start(bf16[3,3,384,256]{3,2,1,0:T(8,128)(2,1)} %copy.17) | copy-start | bytes 5308420
  106.8 0.8 copy-start.6
  107.6 0.8 copy-start.1
where the time goes:
time: 109 us
  waiting for transfers between devices  32.4 us (30%)
  Pallas kernels  22.8 us (21%)
  local copies, waits for them, and re-layouts  22 us (20%)
  other arithmetic  11.3 us (10%)
  starting transfers between devices  9.82 us (9%)
  between operations  9.42 us (9%)
    ppermute x6, waiting for transfers between devices, passed_along(): lax.ppermute(value, axis, [(i, (i + by) % size) for i in range(size)])  32.4 us
    pallas_call x4, Pallas kernels, denoise(): pl.pallas_call(step_kernel, out_shape=jax.ShapeDtypeStruct(block.shape, j...  22.8 us
    ppermute x6, starting transfers between devices, passed_along(): lax.ppermute(value, axis, [(i, (i + by) % size) for i in range(size)])  9.82 us
    unnamed x20, local copies, waits for them, and re-layouts  7.48 us
    concatenate x2, other arithmetic, banded(): jnp.concatenate(columns, axis=3)  7.07 us
    concatenate x2, local copies, waits for them, and re-layouts, banded(): jnp.concatenate(columns, axis=3)  6.51 us
  transfers between devices with their start and end apart: 6, of which 6 were waited for; matrix products, arithmetic and copies ran while one was open for 1% of the time, Pallas kernels for 0%

commit v1 on v0

v1 whole, which is shorter than its diff:
```python
import functools
import math

import jax
import jax.numpy as jnp
from jax import lax
from jax.experimental import pallas as pl
from jax.experimental.pallas import tpu as pltpu
from jax.sharding import PartitionSpec as P

SPAN = 4


def passed_along(value, axis, by):
    size = lax.axis_size(axis)
    return lax.ppermute(value, axis, [(i, (i + by) % size) for i in range(size)])


def prepare_kernel(
    offsets_hbm, timesteps_hbm, first_hbm, second_hbm, time_hbm, latent_hbm,
    *refs,
):
    count = timesteps_hbm.shape[0]
    pick_refs, cut_refs, delta_refs = refs[: count + 1], refs[count + 1 : 2 * count + 1], refs[2 * count + 1 : 3 * count + 1]
    bias_ref, block_ref, first_out, second_out = refs[3 * count + 1 : 3 * count + 5]
    offsets, timesteps, first, second, time_weight, sems = refs[3 * count + 5 :]

    copies = [
        pltpu.make_async_copy(source, target, sems.at[i])
        for i, (source, target) in enumerate(
            (
                (offsets_hbm, offsets),
                (timesteps_hbm, timesteps),
                (first_hbm, first),
                (second_hbm, second),
                (time_hbm, time_weight),
                (latent_hbm, block_ref),
            )
        )
    ]
    for copy in copies:
        copy.start()

    def build(source, target):
        channels, depth = source.shape[2:]
        for tap in range(9):
            taps = source[tap // 3, tap % 3].astype(jnp.float32)
            taps = jnp.concatenate([taps, jnp.zeros_like(taps)], axis=0).T
            moved = pltpu.roll(taps, channels, 1)
            edge = jnp.zeros((channels, 2 * channels), jnp.float32)
            pair = jnp.concatenate([taps, edge], axis=0) + jnp.concatenate([edge, moved], axis=0)
            rows = 4 * channels
            target[pl.ds(tap * rows, rows), :] = pair.astype(jnp.bfloat16)

    for i, (source, out) in enumerate(((first, first_out), (second, second_out))):
        copies[2 + i].wait()
        build(source, out)

    copies[0].wait()
    copies[1].wait()
    before = [0, 0, 0]
    for step in range(count + 1):
        now = [offsets[step, axis] for axis in range(3)] if step < count else [0, 0, 0]
        pick = (now[1] - before[1] + 1) * 3 + now[2] - before[2] + 1
        pick_refs[step][0] = pick * 2 + now[0] if step < count else pick
        before = now
        if step < count:
            cut_refs[step][0] = now[0]
            later = timesteps[step + 1] if step + 1 < count else 0
            delta_refs[step][0] = (later - timesteps[step]).astype(jnp.float32) / 1000.0

    copies[4].wait()
    channels = time_weight.shape[0]
    half_c = channels // 2
    shape = (bias_ref.shape[0], channels)
    place = lax.broadcasted_iota(jnp.int32, shape, 1)
    line = lax.broadcasted_iota(jnp.int32, shape, 0)
    which = jnp.where(place < half_c, place, place - half_c).astype(jnp.float32)
    time = jnp.zeros(shape, jnp.float32)
    for step in range(count):
        time = jnp.where(line == step, timesteps[step].astype(jnp.float32), time)
    angles = time * jnp.exp(-math.log(10000.0) * which / half_c)
    emb = jnp.where(place < half_c, jnp.sin(angles), jnp.cos(angles))
    bias = jnp.dot(emb, time_weight[...], precision=lax.Precision.HIGHEST, preferred_element_type=jnp.float32)
    bias_ref[...] = jnp.concatenate([bias] * SPAN, axis=1)
    copies[5].wait()


def prepare(latent, conv_first, conv_second, time_weight, timesteps, offsets):
    count = timesteps.shape[0]
    depth, channels = conv_first.shape[2:]
    first, second = conv_first.transpose(0, 1, 3, 2), conv_second.transpose(0, 1, 3, 2)
    smem = pl.BlockSpec(memory_space=pltpu.SMEM)
    vmem = pl.BlockSpec(memory_space=pltpu.VMEM)
    hbm = pl.BlockSpec(memory_space=pltpu.HBM)
    matrix = (9 * 4 * (depth // 3), 2 * channels)
    ints = lambda n: jax.ShapeDtypeStruct((n,), jnp.int32)
    real = jax.ShapeDtypeStruct((1,), jnp.float32)
    outs = pl.pallas_call(
        prepare_kernel,
        out_shape=[ints(1)] * (count + 1)
        + [ints(1)] * count
        + [real] * count
        + [jax.ShapeDtypeStruct((-(-count // 8) * 8, SPAN * channels), jnp.float32)]
        + [jax.ShapeDtypeStruct(latent.shape, latent.dtype)]
        + [jax.ShapeDtypeStruct(matrix, jnp.bfloat16)] * 2,
        in_specs=[hbm] * 6,
        out_specs=[smem] * (3 * count + 1) + [vmem] * 4,
        scratch_shapes=[
            pltpu.SMEM(offsets.shape, jnp.int32),
            pltpu.SMEM(timesteps.shape, jnp.int32),
            pltpu.VMEM(first.shape, first.dtype),
            pltpu.VMEM(second.shape, second.dtype),
            pltpu.VMEM(time_weight.shape, jnp.float32),
            pltpu.SemaphoreType.DMA((6,)),
        ],
        compiler_params=pltpu.CompilerParams(vmem_limit_bytes=12 << 20),
        name="prepare",
    )(*(pltpu.with_memory_space_constraint(a, pltpu.HBM) for a in (offsets, timesteps, first, second, time_weight, latent)))
    scalars = 3 * count + 1
    return outs[: count + 1], outs[count + 1 : 2 * count + 1], outs[2 * count + 1 : scalars], outs[scalars:]


def step_kernel(
    step, cut_ref, delta_ref, block_ref, bias_ref, first_ref, second_ref, out_ref, in_ref, hid_ref
):
    size_x, size_y, width = out_ref.shape
    band = bias_ref.shape[1]
    channels = band // SPAN
    depth = band + 2 * channels
    groups = width // band
    half = size_x // 2
    cut = cut_ref[0]
    is_cut = cut == 1

    def spread(values):
        count = values.shape[0]
        edge = jnp.zeros((count, size_y, channels), jnp.float32)
        padded = jnp.concatenate([edge, values, edge], axis=2)
        row = lax.broadcasted_iota(jnp.int32, padded.shape, 1)
        before = jnp.where(row == 0, 0.0, pltpu.roll(padded, 1, 1))
        after = jnp.where(row == size_y - 1, 0.0, pltpu.roll(padded, size_y - 1, 1))
        return [v.astype(jnp.bfloat16) for v in (before, padded, after)]

    def put(ref, start, values):
        for tap, piece in enumerate(spread(values)):
            ref[tap, pl.ds(start, values.shape[0])] = piece

    def widened(ref):
        rows = 4 * channels
        blank = jnp.zeros((2 * channels, 2 * channels), jnp.bfloat16)
        parts = []
        for tap in range(9):
            upper, lower = ref[pl.ds(tap * rows, rows // 2), :], ref[pl.ds(tap * rows + rows // 2, rows // 2), :]
            parts += [
                jnp.concatenate([upper, blank], axis=1),
                jnp.concatenate([lower, upper], axis=1),
                jnp.concatenate([blank, lower], axis=1),
            ]
        return jnp.concatenate(parts, axis=0)

    def convolve(ref, start, count, weight_ref, group):
        rows = []
        for tap in range(9):
            piece = ref[tap % 3, pl.ds(start + tap // 3, count), :, pl.ds(group * band, depth)]
            rows.append(piece.reshape(count * size_y, depth))
        return jnp.dot(jnp.concatenate(rows, axis=1), widened(weight_ref), preferred_element_type=jnp.float32)

    blank = jnp.zeros((3, 1, size_y, width + 2 * channels), jnp.bfloat16)
    in_ref[:, pl.ds(half + 2, 1)] = blank
    put(in_ref, 0, jnp.where(is_cut, block_ref[pl.ds(size_x, 2)], 0.0))
    put(in_ref, 2, block_ref[pl.ds(0, half)])
    put(in_ref, half + 2 + cut, block_ref[pl.ds(half, half)])
    put(in_ref, size_x + 2 + cut, jnp.where(is_cut, block_ref[pl.ds(size_x + 2, 2)], 0.0))

    hid_ref[:, pl.ds(half + 1, 1)] = blank
    bias = bias_ref[pl.ds(step, 1)]
    for side in range(2):
        start = 0 if side == 0 else half + 1 + cut
        pieces = []
        for group in range(groups):
            value = convolve(in_ref, start, half + 1, first_ref, group) + bias
            pieces.append(value / (1.0 + jnp.exp(-value)))
        hidden = jnp.concatenate(pieces, axis=1).reshape(half + 1, size_y, width)
        plane = lax.broadcasted_iota(jnp.int32, hidden.shape, 0)
        hidden = jnp.where((plane != (0 if side == 0 else half)) | is_cut, hidden, 0.0)
        put(hid_ref, start, hidden)

    for side in range(2):
        start = 0 if side == 0 else half + cut
        for group in range(groups):
            noise = convolve(hid_ref, start, half, second_ref, group).reshape(half, size_y, band)
            where = (pl.ds(side * half, half), slice(None), pl.ds(group * band, band))
            out_ref[where] = block_ref[where] + delta_ref[0] * noise


def denoise(step, cut, delta, block, bias, first, second):
    size_x, size_y, width = block.shape
    size_x -= 4
    channels = bias.shape[1] // SPAN
    smem = pl.BlockSpec(memory_space=pltpu.SMEM)
    vmem = pl.BlockSpec(memory_space=pltpu.VMEM)
    return pl.pallas_call(
        functools.partial(step_kernel, step),
        out_shape=jax.ShapeDtypeStruct((size_x, size_y, width), jnp.float32),
        in_specs=[smem, smem, vmem, vmem, vmem, vmem],
        out_specs=vmem,
        scratch_shapes=[
            pltpu.VMEM((3, size_x + 5, size_y, width + 2 * channels), jnp.bfloat16),
            pltpu.VMEM((3, size_x + 3, size_y, width + 2 * channels), jnp.bfloat16),
        ],
        compiler_params=pltpu.CompilerParams(vmem_limit_bytes=12 << 20),
        cost_estimate=pl.CostEstimate(flops=8000000000, bytes_accessed=60000000, transcendentals=0),
        name="denoise",
    )(cut, delta, pltpu.with_memory_space_constraint(block, pltpu.VMEM), bias, *(pltpu.with_memory_space_constraint(a, pltpu.VMEM) for a in (first, second)))


def slide(block, move, axis_name, axis):
    half = block.shape[axis] // 2
    lower = lax.slice_in_dim(block, 0, half, axis=axis)
    upper = lax.slice_in_dim(block, half, 2 * half, axis=axis)
    if move < 0:
        return jnp.concatenate([passed_along(upper, axis_name, 1), lower], axis)
    return jnp.concatenate([upper, passed_along(lower, axis_name, -1)], axis)


def fetch_halo(block):
    length = block.shape[0]
    size = lax.axis_size("gx")
    if size == 2:
        ends = jnp.concatenate([block[length - 2 :], block[:2]], 0)
        return passed_along(ends, "gx", 1)
    return jnp.concatenate([passed_along(block[length - 2 :], "gx", 1), passed_along(block[:2], "gx", -1)], 0)


def choose(index, branches, value):
    traced = jax.make_jaxpr(lambda i, v: lax.switch(i, branches, v))(index, value)
    (call,) = [e for e in traced.jaxpr.eqns if e.primitive is lax.cond_p]
    assert len(call.invars) == 2 and not traced.consts
    outs = lax.cond_p.bind(index, value, **call.params)
    return outs[0] if len(outs) == 1 else outs


def exchange(block, pick, last):
    def branch(y, z, x):
        def run(values):
            if z:
                values = slide(values, z, "gz", 2)
            if y:
                values = slide(values, y, "gy", 1)
            if x is None:
                return values
            halo = fetch_halo(values) if x else jnp.zeros((4,) + values.shape[1:], jnp.float32)
            return jnp.concatenate([values, halo], 0)

        return run

    moves = (-1, 0, 1)
    ends = (None,) if last else (0, 1)
    branches = [branch(y, z, x) for y in moves for z in moves for x in ends]
    return choose(pick.reshape(()), branches, block)


def shards(latent, conv_first, conv_second, time_weight, timesteps, offsets):
    count = timesteps.shape[0]
    picks, cuts, deltas, rest = prepare(latent, conv_first, conv_second, time_weight, timesteps, offsets)
    bias, block, first, second = rest
    for step in range(count):
        block = exchange(block, picks[step], False)
        block = denoise(step, cuts[step], deltas[step], block, bias, first, second)
    return exchange(block, picks[count], True)


def solution(mesh):
    return jax.shard_map(
        shards,
        mesh=mesh,
        in_specs=(P("gx", "gy", "gz"), P(), P(), P(), P(), P()),
        out_specs=P("gx", "gy", "gz"),
        check_vma=False,
    )
```

time: 109 us -> 62.9 us (0.58)
  local copies, waits for them, and re-layouts: 22 us -> 0.97 us
  other arithmetic: 11.3 us -> 0.28 us
  between operations: 9.42 us -> 0.09 us
  Pallas kernels: 22.8 us -> 18.7 us
  loops' own time: 0.86 us -> 3.89 us
  waiting for transfers between devices: 32.4 us -> 29.9 us
    concatenate x2, other arithmetic: 7.07 us -> 0.09 us  [run(): return jnp.concatenate([values, halo], 0)]
    unnamed x20 -> x2, local copies, waits for them, and re-layouts: 7.48 us -> 0.79 us
    concatenate x2 -> x0, local copies, waits for them, and re-layouts: 6.51 us -> none  [banded(): jnp.concatenate(columns, axis=3)]
    pallas_call x4 -> x5, Pallas kernels: 22.8 us -> 18.7 us  [the longest x4 16.1 us: denoise(): pl.pallas_call(functools.partial(step_kernel, step), out_shape=jax.ShapeD...]
    slice x5 -> x0, local copies, waits for them, and re-layouts: 3.48 us -> none  [the longest x1 1.41 us: shards(): cut = offsets[step, 0]]
    another operation x5, loops' own time: 0.86 us -> 3.89 us  [choose(): outs = lax.cond_p.bind(index, value, **call.params)]
    ppermute x6, waiting for transfers between devices: 32.4 us -> 29.9 us  [passed_along(): lax.ppermute(value, axis, [(i, (i + by) % size) for i in range(size)])]
    another operation x10 -> x0, local copies, waits for them, and re-layouts: 1.67 us -> none
  transfers between devices with their start and end apart: 6 -> 6, of which waited for: 6 -> 6; matrix products, arithmetic and copies ran while one was open for 1% -> 0% of each run, Pallas kernels for 0% -> 0%
where the time goes in v1:
time: 62.9 us; the launch traced here: 63.7 us
  waiting for transfers between devices  29.9 us (48%)
  Pallas kernels  18.7 us (30%)
  starting transfers between devices  9.84 us (16%)
  loops' own time  3.89 us (6%)
  local copies, waits for them, and re-layouts  0.97 us (2%)
    ppermute x6, waiting for transfers between devices, passed_along(): lax.ppermute(value, axis, [(i, (i + by) % size) for i in range(size)])  29.9 us
    pallas_call x4, Pallas kernels, denoise(): pl.pallas_call(functools.partial(step_kernel, step), out_shape=jax.ShapeD...  16.1 us
    ppermute x6, starting transfers between devices, passed_along(): lax.ppermute(value, axis, [(i, (i + by) % size) for i in range(size)])  9.84 us
    another operation x5, loops' own time, choose(): outs = lax.cond_p.bind(index, value, **call.params)  3.89 us
    pallas_call x1, Pallas kernels, prepare(): pl.pallas_call(prepare_kernel, out_shape=[ints(1)] * (count + 1) + [ints(...  2.61 us
  transfers between devices with their start and end apart: 6, of which 6 were waited for; matrix products, arithmetic and copies ran while one was open for 0% of the time, Pallas kernels for 0%

profile of v1, /device:TPU:0, one launch (start us, length us, event | category | flops | bytes accessed | tf_op | source)
XLA Modules:
  0.0 63.7 jit_solution(15626273908784658243)
XLA Ops:
  0.0 2.6 %prepare.1 = (s32[1]{0:T(128)}, s32[1]{0:T(128)}, s32[1]{0:T(128)}, s32[1]{0:T(128)}, s32[1]{0:T(128)}, /*index=5*/s32[1]{0:T(128)}, s32[1]{0:T(128)}, s32[1]{0:...) custom-call(s32[4,3]{1,0:T(4,128)} %offsets_hbm.1, ...), custom_call_target="tpu_custom_call" | custom-call | tf_op jit(solution)/shard_map/prepare/pallas_call | solution.py:99
  2.6 13.5 %conditional.5 = (f32[20,16,512]{2,1,0:T(8,128)S(1)}) conditional(s32[]{:T(128)} %bitcast.6, f32[16,16,512]{2,1,0:T(8,128)S(1)} %get-tuple-element.202, f32[16,16,512]{2,1,0:T(8,128)S(1)} %get-tuple-element.202, f32[16,16,512]{2,1,0:T(8,128)S(1)} %get-tuple-element.202, ...), branch_computations={%region_0.0_spmd, %region_1.0_spmd, %region_2.0_spmd, %region_3.0_... | conditional | flops 1048576 | bytes 6684800 | solution.py:240
  3.4 2.5 %collective-permute-start.26 = (f32[16,8,512]{2,1,0:T(8,128)S(1)}, f32[16,8,512]{2,1,0:T(8,128)S(1)}, u32[]{:S(2)}, u32[]{:S(2)}) collective-permute-start(f32[16,8,512]{2,1,0:T(8,128)S(1)} %get-tuple-element.244), channel_id=1, source_target_pairs={{0,12},{4,0},{8,4},{12,8},{1,13},{5,1},{9,5},{13,9},{2,14},{6,2},{... | collective-permute-start | bytes 786440 | tf_op jit(solution)/shard_map/cond/branch_15_fun/ppermute | solution.py:16
  5.8 3.9 %collective-permute-done.26 = f32[16,8,512]{2,1,0:T(8,128)S(1)} collective-permute-done((f32[16,8,512]{2,1,0:T(8,128)S(1)}, f32[16,8,512]{2,1,0:T(8,128)S(1)}, u32[]{:S(2)}, u32[]{:S(2)}) %collective-permute-start.26) | collective-permute-done | bytes 262176 | tf_op jit(solution)/shard_map/cond/branch_15_fun/ppermute | solution.py:16
  9.7 1.6 %collective-permute-start.27 = (f32[4,16,512]{2,1,0:T(8,128)S(1)}, f32[4,16,512]{2,1,0:T(8,128)S(1)}, u32[]{:S(2)}, u32[]{:S(2)}) collective-permute-start(f32[4,16,512]{2,1,0:T(8,128)S(1)} %fusion.18), channel_id=1, source_target_pairs={{0,16},{16,0},{1,17},{17,1},{2,18},{18,2},{3,19},{19,3},{4,20},{20... | collective-permute-start | bytes 393224 | tf_op jit(solution)/shard_map/cond/branch_15_fun/ppermute | solution.py:16
  11.3 4.7 %collective-permute-done.27 = f32[4,16,512]{2,1,0:T(8,128)S(1)} collective-permute-done((f32[4,16,512]{2,1,0:T(8,128)S(1)}, f32[4,16,512]{2,1,0:T(8,128)S(1)}, u32[]{:S(2)}, u32[]{:S(2)}) %collective-permute-start.27) | collective-permute-done | bytes 131104 | tf_op jit(solution)/shard_map/cond/branch_15_fun/ppermute | solution.py:16
  16.1 4.1 %denoise.4 = f32[16,16,512]{2,1,0:T(8,128)S(1)} custom-call(s32[1]{0:T(128)} %get-tuple-element.199.cut_ref, f32[1]{0:T(128)} %get-tuple-element.200.delta_ref, f32[20,16,512]{2,1,0:T(8,128)S(1)} %get-tuple-element.420.block_ref, f32[8,256]{1,0:T(8,128)S(1)} %get-tuple-element.203.bias_ref, bf16[2304,128]{1,0:T(8,128)(2,1)S(1)} %get-tuple-element.204.first_ref, ...), custom_call_target="tpu_custom_call" | custom-call | flops 8000000000 | bytes 60000000 | tf_op jit(solution)/shard_map/denoise/pallas_call | solution.py:203
  20.2 6.9 %conditional.6 = (f32[20,16,512]{2,1,0:T(8,128)S(1)}) conditional(s32[]{:T(128)} %bitcast.5, f32[16,16,512]{2,1,0:T(8,128)S(1)} %denoise.4, f32[16,16,512]{2,1,0:T(8,128)S(1)} %denoise.4, f32[16,16,512]{2,1,0:T(8,128)S(1)} %denoise.4, f32[16,16,512]{2,1,0:T(8,128)S(1)} %denoise.4, ...), branch_computations={%region_18.0_spmd, %region_19.0_spmd, %region_20.0_spmd, %region_2... | conditional | flops 1048576 | bytes 6684800 | solution.py:240
  20.9 0.1 collective-permute-start.38
  21.0 5.8 %collective-permute-done.38 = f32[16,8,512]{2,1,0:T(8,128)S(1)} collective-permute-done((f32[16,8,512]{2,1,0:T(8,128)S(1)}, f32[16,8,512]{2,1,0:T(8,128)S(1)}, u32[]{:S(2)}, u32[]{:S(2)}) %collective-permute-start.38) | collective-permute-done | bytes 262176 | tf_op jit(solution)/shard_map/cond/branch_2_fun/ppermute | solution.py:16
  26.8 0.1 select_maximum_fusion.9
  27.1 4.1 %denoise.5 = f32[16,16,512]{2,1,0:T(8,128)S(1)} custom-call(s32[1]{0:T(128)} %get-tuple-element.196.cut_ref, f32[1]{0:T(128)} %get-tuple-element.197.delta_ref, f32[20,16,512]{2,1,0:T(8,128)S(1)} %get-tuple-element.421.block_ref, f32[8,256]{1,0:T(8,128)S(1)} %get-tuple-element.203.bias_ref, bf16[2304,128]{1,0:T(8,128)(2,1)S(1)} %get-tuple-element.204.first_ref, ...), custom_call_target="tpu_custom_call" | custom-call | flops 8000000000 | bytes 60000000 | tf_op jit(solution)/shard_map/denoise/pallas_call | solution.py:203
  31.1 8.4 %conditional.7 = (f32[20,16,512]{2,1,0:T(8,128)S(1)}) conditional(s32[]{:T(128)} %bitcast.4, f32[16,16,512]{2,1,0:T(8,128)S(1)} %denoise.5, f32[16,16,512]{2,1,0:T(8,128)S(1)} %denoise.5, f32[16,16,512]{2,1,0:T(8,128)S(1)} %denoise.5, f32[16,16,512]{2,1,0:T(8,128)S(1)} %denoise.5, ...), branch_computations={%region_36.0_spmd, %region_37.0_spmd, %region_38.0_spmd, %region_3... | conditional | flops 1048576 | bytes 6684800 | solution.py:240
  31.8 0.1 fusion.137
  31.9 3.7 %collective-permute-start.83 = (f32[16,16,256]{2,1,0:T(8,128)S(1)}, f32[16,16,256]{2,1,0:T(8,128)S(1)}, u32[]{:S(2)}, u32[]{:S(2)}) collective-permute-start(f32[16,16,256]{2,1,0:T(8,128)S(1)} %get-tuple-element.322), channel_id=1, source_target_pairs={{0,3},{1,0},{2,1},{3,2},{4,7},{5,4},{6,5},{7,6},{8,11},{9,8},{10,9... | collective-permute-start | bytes 786440 | tf_op jit(solution)/shard_map/cond/branch_10_fun/ppermute | solution.py:16
  35.5 3.9 %collective-permute-done.83 = f32[16,16,256]{2,1,0:T(8,128)S(1)} collective-permute-done((f32[16,16,256]{2,1,0:T(8,128)S(1)}, f32[16,16,256]{2,1,0:T(8,128)S(1)}, u32[]{:S(2)}, u32[]{:S(2)}) %collective-permute-start.83) | collective-permute-done | bytes 262176 | tf_op jit(solution)/shard_map/cond/branch_10_fun/ppermute | solution.py:16
  39.4 0.1 select_maximum_fusion.20
  39.5 4.0 %denoise.6 = f32[16,16,512]{2,1,0:T(8,128)S(1)} custom-call(s32[1]{0:T(128)} %get-tuple-element.193.cut_ref, f32[1]{0:T(128)} %get-tuple-element.194.delta_ref, f32[20,16,512]{2,1,0:T(8,128)S(1)} %get-tuple-element.422.block_ref, f32[8,256]{1,0:T(8,128)S(1)} %get-tuple-element.203.bias_ref, bf16[2304,128]{1,0:T(8,128)(2,1)S(1)} %get-tuple-element.204.first_ref, ...), custom_call_target="tpu_custom_call" | custom-call | flops 8000000000 | bytes 60000000 | tf_op jit(solution)/shard_map/denoise/pallas_call | solution.py:203
  43.5 6.0 %conditional.8 = (f32[20,16,512]{2,1,0:T(8,128)S(1)}) conditional(s32[]{:T(128)} %bitcast.3, f32[16,16,512]{2,1,0:T(8,128)S(1)} %denoise.6, f32[16,16,512]{2,1,0:T(8,128)S(1)} %denoise.6, f32[16,16,512]{2,1,0:T(8,128)S(1)} %denoise.6, f32[16,16,512]{2,1,0:T(8,128)S(1)} %denoise.6, ...), branch_computations={%region_54.0_spmd, %region_55.0_spmd, %region_56.0_spmd, %region_5... | conditional | flops 1048576 | bytes 6684800 | solution.py:240
  44.3 1.6 %collective-permute-start.115 = (f32[4,16,512]{2,1,0:T(8,128)S(1)}, f32[4,16,512]{2,1,0:T(8,128)S(1)}, u32[]{:S(2)}, u32[]{:S(2)}) collective-permute-start(f32[4,16,512]{2,1,0:T(8,128)S(1)} %pad_maximum_fusion.111), channel_id=1, source_target_pairs={{0,16},{16,0},{1,17},{17,1},{2,18},{18,2},{3,19},{19,3},{4,20},{20... | collective-permute-start | bytes 393224 | tf_op jit(solution)/shard_map/cond/branch_9_fun/ppermute | solution.py:16
  45.9 3.5 %collective-permute-done.115 = f32[4,16,512]{2,1,0:T(8,128)S(1)} collective-permute-done((f32[4,16,512]{2,1,0:T(8,128)S(1)}, f32[4,16,512]{2,1,0:T(8,128)S(1)}, u32[]{:S(2)}, u32[]{:S(2)}) %collective-permute-start.115) | collective-permute-done | bytes 131104 | tf_op jit(solution)/shard_map/cond/branch_9_fun/ppermute | solution.py:16
  49.4 4.0 %denoise.7 = f32[16,16,512]{2,1,0:T(8,128)S(1)} custom-call(s32[1]{0:T(128)} %get-tuple-element.190.cut_ref, f32[1]{0:T(128)} %get-tuple-element.191.delta_ref, f32[20,16,512]{2,1,0:T(8,128)S(1)} %get-tuple-element.423.block_ref, f32[8,256]{1,0:T(8,128)S(1)} %get-tuple-element.203.bias_ref, bf16[2304,128]{1,0:T(8,128)(2,1)S(1)} %get-tuple-element.204.first_ref, ...), custom_call_target="tpu_custom_call" | custom-call | flops 8000000000 | bytes 60000000 | tf_op jit(solution)/shard_map/denoise/pallas_call | solution.py:203
  53.4 9.5 %conditional.9 = (f32[16,16,512]{2,1,0:T(8,128)S(1)}) conditional(s32[]{:T(128)} %bitcast.2, f32[16,16,512]{2,1,0:T(8,128)S(1)} %denoise.7, f32[16,16,512]{2,1,0:T(8,128)S(1)} %denoise.7, f32[16,16,512]{2,1,0:T(8,128)S(1)} %denoise.7, f32[16,16,512]{2,1,0:T(8,128)S(1)} %denoise.7, ...), branch_computations={%region_72.0_spmd, %region_73.0_spmd, %region_74.0_spmd, %region_7... | conditional | flops 327680 | bytes 5242968 | solution.py:240
  54.1 0.1 fusion.165
  54.1 0.5 collective-permute-start.137
  54.6 8.2 %collective-permute-done.137 = f32[16,16,256]{2,1,0:T(8,128)S(1)} collective-permute-done((f32[16,16,256]{2,1,0:T(8,128)S(1)}, f32[16,16,256]{2,1,0:T(8,128)S(1)}, u32[]{:S(2)}, u32[]{:S(2)}) %collective-permute-start.137) | collective-permute-done | bytes 262176 | tf_op jit(solution)/shard_map/cond/branch_3_fun/ppermute | solution.py:16
  62.9 0.0 copy-start
  62.9 0.8 %copy-done = f32[16,16,512]{2,1,0:T(8,128)} copy-done((f32[16,16,512]{2,1,0:T(8,128)}, f32[16,16,512]{2,1,0:T(8,128)S(1)}, u32[]{:S(2)}) %copy-start) | copy-done | bytes 524312
  (8 shorter events, 0.2 us)
Async XLA Ops:
  3.4 6.3 %collective-permute-start.26 = (f32[16,8,512]{2,1,0:T(8,128)S(1)}, f32[16,8,512]{2,1,0:T(8,128)S(1)}, u32[]{:S(2)}, u32[]{:S(2)}) collective-permute-start(f32[16,8,512]{2,1,0:T(8,128)S(1)} %get-tuple-element.244), channel_id=1, source_target_pairs={{0,12},{4,0},{8,4},{12,8},{1,13},{5,1},{9,5},{13,9},{2,14},{6,2},{... | collective-permute-start | bytes 786440 | tf_op jit(solution)/shard_map/cond/branch_15_fun/ppermute | solution.py:16
  9.7 6.3 %collective-permute-start.27 = (f32[4,16,512]{2,1,0:T(8,128)S(1)}, f32[4,16,512]{2,1,0:T(8,128)S(1)}, u32[]{:S(2)}, u32[]{:S(2)}) collective-permute-start(f32[4,16,512]{2,1,0:T(8,128)S(1)} %fusion.18), channel_id=1, source_target_pairs={{0,16},{16,0},{1,17},{17,1},{2,18},{18,2},{3,19},{19,3},{4,20},{20... | collective-permute-start | bytes 393224 | tf_op jit(solution)/shard_map/cond/branch_15_fun/ppermute | solution.py:16
  20.9 5.8 %collective-permute-start.38 = (f32[16,8,512]{2,1,0:T(8,128)S(1)}, f32[16,8,512]{2,1,0:T(8,128)S(1)}, u32[]{:S(2)}, u32[]{:S(2)}) collective-permute-start(f32[16,8,512]{2,1,0:T(8,128)S(1)} %get-tuple-element.259), channel_id=1, source_target_pairs={{0,4},{4,8},{8,12},{12,0},{1,5},{5,9},{9,13},{13,1},{2,6},{6,10},{... | collective-permute-start | bytes 786440 | tf_op jit(solution)/shard_map/cond/branch_2_fun/ppermute | solution.py:16
  31.9 7.6 %collective-permute-start.83 = (f32[16,16,256]{2,1,0:T(8,128)S(1)}, f32[16,16,256]{2,1,0:T(8,128)S(1)}, u32[]{:S(2)}, u32[]{:S(2)}) collective-permute-start(f32[16,16,256]{2,1,0:T(8,128)S(1)} %get-tuple-element.322), channel_id=1, source_target_pairs={{0,3},{1,0},{2,1},{3,2},{4,7},{5,4},{6,5},{7,6},{8,11},{9,8},{10,9... | collective-permute-start | bytes 786440 | tf_op jit(solution)/shard_map/cond/branch_10_fun/ppermute | solution.py:16
  44.3 5.0 %collective-permute-start.115 = (f32[4,16,512]{2,1,0:T(8,128)S(1)}, f32[4,16,512]{2,1,0:T(8,128)S(1)}, u32[]{:S(2)}, u32[]{:S(2)}) collective-permute-start(f32[4,16,512]{2,1,0:T(8,128)S(1)} %pad_maximum_fusion.111), channel_id=1, source_target_pairs={{0,16},{16,0},{1,17},{17,1},{2,18},{18,2},{3,19},{19,3},{4,20},{20... | collective-permute-start | bytes 393224 | tf_op jit(solution)/shard_map/cond/branch_9_fun/ppermute | solution.py:16
  54.1 8.7 %collective-permute-start.137 = (f32[16,16,256]{2,1,0:T(8,128)S(1)}, f32[16,16,256]{2,1,0:T(8,128)S(1)}, u32[]{:S(2)}, u32[]{:S(2)}) collective-permute-start(f32[16,16,256]{2,1,0:T(8,128)S(1)} %get-tuple-element.397), channel_id=1, source_target_pairs={{0,1},{1,2},{2,3},{3,0},{4,5},{5,6},{6,7},{7,4},{8,9},{9,10},{10,1... | collective-permute-start | bytes 786440 | tf_op jit(solution)/shard_map/cond/branch_3_fun/ppermute | solution.py:16
  62.9 0.8 %copy-start = (f32[16,16,512]{2,1,0:T(8,128)}, f32[16,16,512]{2,1,0:T(8,128)S(1)}, u32[]{:S(2)}) copy-start(f32[16,16,512]{2,1,0:T(8,128)S(1)} %get-tuple-element.424) | copy-start | bytes 1572868
